TPU v7x, 32 devices: a whole 2x2x4 slice. The times are simulated.
32 devices in a mesh: wide: 8 (over y, x, core), narrow: 4 (over z).
Axes of the slice: x: 2, y: 2, z: 4, core: 2. Of those that a mesh axis runs over, the one named last changes fastest.
Arguments:
- layer_input: bfloat16 [2, 8, 256, 2048], P(None, 'wide', 'narrow'), may hold values from -6 to 6
- document_lengths: int32 [2, 8, 4], P(None, 'wide'), may hold values from 1 to 128, 256 in all within a row
- attn_gain: bfloat16 [2048], replicated, may hold values from 0.5 to 1.5
- w_query: bfloat16 [2048, 2048], P(None, 'narrow'), may hold values from -0.125 to 0.125
- w_key: bfloat16 [2048, 1024], P(None, 'narrow'), may hold values from -0.125 to 0.125
- w_value: bfloat16 [2048, 1024], P(None, 'narrow'), may hold values from -0.125 to 0.125
- query_gain: bfloat16 [128], replicated, may hold values from 1 to 2.5
- key_gain: bfloat16 [128], replicated, may hold values from 1 to 2.5
- w_out: bfloat16 [2048, 2048], P('narrow'), may hold values from -0.75 to 0.75
- mlp_gain: bfloat16 [2048], replicated, may hold values from 0.5 to 1.5
- w_gate: bfloat16 [2048, 6144], P(None, 'narrow'), may hold values from -0.125 to 0.125
- w_up: bfloat16 [2048, 6144], P(None, 'narrow'), may hold values from -0.125 to 0.125
- w_down: bfloat16 [6144, 2048], P('narrow'), may hold values from -0.078125 to 0.078125
- output_cotangent: bfloat16 [2, 8, 256, 2048], P(None, 'wide', 'narrow'), may hold values from -6 to 6
Outputs:
- layer_out: float32 [2, 8, 256, 2048], P(None, 'wide', 'narrow')
- in_grad: float32 [2, 8, 256, 2048], P(None, 'wide', 'narrow')
- attn_gain_grad: float32 [2048], replicated
- w_query_grad: float32 [2048, 2048], P('wide', 'narrow')
- w_key_grad: float32 [2048, 1024], P('wide', 'narrow')
- w_value_grad: float32 [2048, 1024], P('wide', 'narrow')
- query_gain_grad: float32 [128], replicated
- key_gain_grad: float32 [128], replicated
- w_out_grad: float32 [2048, 2048], P('narrow', 'wide')
- mlp_gain_grad: float32 [2048], replicated
- w_gate_grad: float32 [2048, 6144], P('wide', 'narrow')
- w_up_grad: float32 [2048, 6144], P('wide', 'narrow')
- w_down_grad: float32 [6144, 2048], P('narrow', 'wide')
Inputs may be any that keep to these rules, and one draw needn't show every extreme that they name: `document_lengths`: each row's 4 document lengths sum to 256, and in every row the longest is exactly 128.
All inputs are finite; a program needn't handle non-finite values.
Results may differ from a plain program's by a relative error of at most 0.013.
The roundings to bfloat16 on the way count: a program that leaves them out, or rounds other values in their place, can miss the bound.
Values may be sent and summed in bfloat16 or wider, within the bound.
A program may use at most 192 MiB of HBM per device.

v0:
```python
import jax
import jax.numpy as jnp
from jax import lax
from jax.sharding import PartitionSpec as P

norm_eps = 1e-06
masked_score = -1e30


def rms_scale(values):
    return lax.rsqrt(jnp.mean(values * values, axis=-1, keepdims=True) + norm_eps)


def rms_back(grad_in, normed_hat, scale_rows):
    return scale_rows * (
        grad_in - normed_hat * jnp.mean(grad_in * normed_hat, axis=-1, keepdims=True)
    )


def doc_layout(lengths, seq_len):
    doc_ends = jnp.cumsum(lengths)
    starts = doc_ends - lengths
    places = lax.iota(jnp.int32, seq_len)
    segment = jnp.sum((places[:, None] >= doc_ends[None, :]).astype(jnp.int32), axis=1)
    member = segment[:, None] == lax.iota(jnp.int32, lengths.shape[0])[None, :]
    doc_first = jnp.sum(jnp.where(member, starts[None, :], 0), axis=1)
    allowed = (segment[:, None] == segment[None, :]) & (places[None, :] <= places[:, None])
    return (places - doc_first, allowed)


def rope_tables(inside, head_dim):
    half_dim = head_dim // 2
    frequency = jnp.power(1000000.0, -2.0 * lax.iota(jnp.float32, half_dim) / head_dim)
    angles = inside.astype(jnp.float32)[:, None] * frequency[None, :]
    return (jnp.cos(angles), jnp.sin(angles))


def rotate(values, cos_table, sine_table):
    half_dim = values.shape[-1] // 2
    first_half = values[..., :half_dim]
    second = values[..., half_dim:]
    cos_wide = cos_table[:, None, :]
    sine_wide = sine_table[:, None, :]
    return jnp.concatenate(
        [first_half * cos_wide - second * sine_wide, second * cos_wide + first_half * sine_wide],
        axis=-1,
    )


def contract_rows(left_side, right_side):
    return lax.dot_general(
        left_side, right_side, (((0,), (0,)), ((), ())), preferred_element_type=jnp.float32
    )


def contract_cols(left_side, right_side):
    return lax.dot_general(
        left_side, right_side, (((1,), (1,)), ((), ())), preferred_element_type=jnp.float32
    )


def row_product(source, weight):
    return jnp.dot(source, weight, preferred_element_type=jnp.float32)


def row_back_product(source, weight):
    return contract_cols(source, weight)


def attention_scores(grouped, key_rot, allowed, score_scale):
    raw_scores = (
        jnp.einsum("tkgd,ukd->kgtu", grouped, key_rot, preferred_element_type=jnp.float32)
        * score_scale
    )
    return jnp.where(allowed[None, None], raw_scores, masked_score)


def local(
    layer_input,
    document_lengths,
    attn_gain,
    w_query,
    w_key,
    w_value,
    query_gain,
    key_gain,
    w_out,
    mlp_gain,
    w_gate,
    w_up,
    w_down,
    output_cotangent,
):
    shard_rows = layer_input.shape[2]
    seq_len = shard_rows * lax.axis_size("narrow")
    head_dim = query_gain.shape[0]
    query_cols = w_query.shape[1]
    key_cols = w_key.shape[1]
    query_heads = query_cols // head_dim
    kv_local = key_cols // head_dim
    group_size = query_cols // key_cols
    ff_cols = w_gate.shape[1]
    score_scale = head_dim ** (-0.5)
    w_qkv = jnp.concatenate([w_query, w_key, w_value], axis=1)
    w_both = jnp.concatenate([w_gate, w_up], axis=1)
    attn_gain_f = attn_gain.astype(jnp.float32)
    query_gain_f = query_gain.astype(jnp.float32)
    key_gain_f = key_gain.astype(jnp.float32)
    mlp_gain_f = mlp_gain.astype(jnp.float32)
    totals = None
    small_totals = None
    outputs_list = []
    in_grads = []
    for micro_step in range(layer_input.shape[0]):
        rows_in = layer_input[micro_step, 0].astype(jnp.float32)
        inside, allowed = doc_layout(document_lengths[micro_step, 0], seq_len)
        cos_table, sine_table = rope_tables(inside, head_dim)
        scale_one = rms_scale(rows_in)
        hat_one = rows_in * scale_one
        normed = (hat_one * attn_gain_f).astype(jnp.bfloat16)
        normed_full = lax.all_gather(normed, "narrow", axis=0, tiled=True)
        projected = jnp.dot(normed_full, w_qkv, preferred_element_type=jnp.float32)
        query_raw = projected[:, :query_cols].reshape(seq_len, query_heads, head_dim)
        key_raw = projected[:, query_cols : query_cols + key_cols].reshape(
            seq_len, kv_local, head_dim
        )
        value_rows = (
            projected[:, query_cols + key_cols :]
            .astype(jnp.bfloat16)
            .reshape(seq_len, kv_local, head_dim)
        )
        query_scale = rms_scale(query_raw)
        query_hat = query_raw * query_scale
        query_rot = rotate(query_hat * query_gain_f, cos_table, sine_table).astype(jnp.bfloat16)
        key_scale = rms_scale(key_raw)
        key_hat = key_raw * key_scale
        key_rot = rotate(key_hat * key_gain_f, cos_table, sine_table).astype(jnp.bfloat16)
        grouped = query_rot.reshape(seq_len, kv_local, group_size, head_dim)
        scores = attention_scores(grouped, key_rot, allowed, score_scale)
        top_score = jnp.max(scores, axis=-1, keepdims=True)
        exponent = jnp.exp(scores - top_score)
        total_mass = jnp.sum(exponent, axis=-1, keepdims=True)
        log_mass = top_score + jnp.log(total_mass)
        prob_low = (exponent / total_mass).astype(jnp.bfloat16)
        attn_mix = jnp.einsum(
            "kgtu,ukd->tkgd", prob_low, value_rows, preferred_element_type=jnp.float32
        )
        attn_mix = attn_mix.reshape(seq_len, query_cols).astype(jnp.bfloat16)
        attn_branch = lax.psum_scatter(
            row_product(attn_mix, w_out), "narrow", scatter_dimension=0, tiled=True
        )
        middle = rows_in + attn_branch
        scale_two = rms_scale(middle)
        hat_two = middle * scale_two
        normed_two = (hat_two * mlp_gain_f).astype(jnp.bfloat16)
        normed_two_full = lax.all_gather(normed_two, "narrow", axis=0, tiled=True)
        gate_up = jnp.dot(normed_two_full, w_both, preferred_element_type=jnp.float32)
        gate_pre = gate_up[:, :ff_cols]
        up_proj = gate_up[:, ff_cols:]
        sigmoid_gate = jax.nn.sigmoid(gate_pre)
        silu_gate = gate_pre * sigmoid_gate
        activated = (silu_gate * up_proj).astype(jnp.bfloat16)
        mlp_branch = lax.psum_scatter(
            row_product(activated, w_down).astype(jnp.bfloat16),
            "narrow",
            scatter_dimension=0,
            tiled=True,
        ).astype(jnp.float32)
        outputs_list.append(middle + mlp_branch)
        cot_rows = output_cotangent[micro_step, 0]
        cot_full = lax.all_gather(cot_rows, "narrow", axis=0, tiled=True)
        grad_down = contract_rows(activated, cot_full)
        d_act = contract_cols(cot_full, w_down)
        d_gate = d_act * up_proj * sigmoid_gate * (1.0 + gate_pre * (1.0 - sigmoid_gate))
        d_up = d_act * silu_gate
        d_both = jnp.concatenate([d_gate, d_up], axis=1).astype(jnp.bfloat16)
        grad_both = contract_rows(normed_two_full, d_both)
        d_normed_two = lax.psum_scatter(
            row_back_product(d_both, w_both), "narrow", scatter_dimension=0, tiled=True
        )
        mlp_gain_part = jnp.sum(d_normed_two * hat_two, axis=0)
        d_middle = cot_rows.astype(jnp.float32) + rms_back(
            d_normed_two * mlp_gain_f, hat_two, scale_two
        )
        d_branch = d_middle.astype(jnp.bfloat16)
        d_branch_full = lax.all_gather(d_branch, "narrow", axis=0, tiled=True)
        grad_out = contract_rows(attn_mix, d_branch_full)
        d_mix = contract_cols(d_branch_full, w_out).astype(jnp.bfloat16)
        d_mix = d_mix.reshape(seq_len, kv_local, group_size, head_dim)
        d_prob = jnp.einsum("tkgd,ukd->kgtu", d_mix, value_rows, preferred_element_type=jnp.float32)
        scores_again = attention_scores(grouped, key_rot, allowed, score_scale)
        prob_again = jnp.exp(scores_again - log_mass)
        prob_back_low = prob_again.astype(jnp.bfloat16)
        d_value = jnp.einsum(
            "kgtu,tkgd->ukd", prob_back_low, d_mix, preferred_element_type=jnp.float32
        )
        d_score = prob_again * (d_prob - jnp.sum(prob_again * d_prob, axis=-1, keepdims=True))
        d_score = d_score.astype(jnp.bfloat16)
        d_query = jnp.einsum("kgtu,ukd->tkgd", d_score, key_rot, preferred_element_type=jnp.float32)
        d_query = d_query.reshape(seq_len, query_heads, head_dim) * score_scale
        d_key = (
            jnp.einsum("kgtu,tkgd->ukd", d_score, grouped, preferred_element_type=jnp.float32)
            * score_scale
        )
        d_query_norm = rotate(d_query, cos_table, -sine_table)
        d_key_norm = rotate(d_key, cos_table, -sine_table)
        query_gain_part = jnp.sum(d_query_norm * query_hat, axis=(0, 1))
        key_gain_part = jnp.sum(d_key_norm * key_hat, axis=(0, 1))
        d_query_raw = rms_back(d_query_norm * query_gain_f, query_hat, query_scale)
        d_key_raw = rms_back(d_key_norm * key_gain_f, key_hat, key_scale)
        d_proj = jnp.concatenate(
            [
                d_query_raw.reshape(seq_len, query_cols),
                d_key_raw.reshape(seq_len, key_cols),
                d_value.reshape(seq_len, key_cols),
            ],
            axis=1,
        ).astype(jnp.bfloat16)
        grad_qkv = contract_rows(normed_full, d_proj)
        d_normed = lax.psum_scatter(
            row_back_product(d_proj, w_qkv), "narrow", scatter_dimension=0, tiled=True
        )
        attn_gain_part = jnp.sum(d_normed * hat_one, axis=0)
        in_grads.append(d_middle + rms_back(d_normed * attn_gain_f, hat_one, scale_one))
        grads_now = (grad_qkv, grad_both, grad_out, grad_down)
        small_now = (attn_gain_part, query_gain_part, key_gain_part, mlp_gain_part)
        if totals is None:
            totals = grads_now
            small_totals = small_now
        else:
            totals = tuple((running + extra for running, extra in zip(totals, grads_now)))
            small_totals = tuple(
                (running + extra for running, extra in zip(small_totals, small_now))
            )
    totals = (
        lax.psum_scatter(totals[0], "wide", scatter_dimension=0, tiled=True),
        lax.psum_scatter(totals[1], "wide", scatter_dimension=0, tiled=True),
        lax.psum_scatter(totals[2], "wide", scatter_dimension=1, tiled=True),
        lax.psum_scatter(totals[3], "wide", scatter_dimension=1, tiled=True),
    )
    small_sums = lax.psum(small_totals, ("wide", "narrow"))
    qkv_share, both_share, out_share, down_share = totals
    layer_out = jnp.stack(outputs_list)[:, None]
    in_grad = jnp.stack(in_grads)[:, None]
    return (
        layer_out,
        in_grad,
        small_sums[0],
        qkv_share[:, :query_cols],
        qkv_share[:, query_cols : query_cols + key_cols],
        qkv_share[:, query_cols + key_cols :],
        small_sums[1],
        small_sums[2],
        out_share,
        small_sums[3],
        both_share[:, :ff_cols],
        both_share[:, ff_cols:],
        down_share,
    )


def solution(mesh):
    in_specs = (
        P(None, "wide", "narrow", None),
        P(None, "wide", None),
        P(),
        P(None, "narrow"),
        P(None, "narrow"),
        P(None, "narrow"),
        P(),
        P(),
        P("narrow", None),
        P(),
        P(None, "narrow"),
        P(None, "narrow"),
        P("narrow", None),
        P(None, "wide", "narrow", None),
    )
    out_specs = (
        P(None, "wide", "narrow", None),
        P(None, "wide", "narrow", None),
        P(),
        P("wide", "narrow"),
        P("wide", "narrow"),
        P("wide", "narrow"),
        P(),
        P(),
        P("narrow", "wide"),
        P(),
        P("wide", "narrow"),
        P("wide", "narrow"),
        P("narrow", "wide"),
    )
    return jax.shard_map(local, mesh=mesh, in_specs=in_specs, out_specs=out_specs, check_vma=False)
```

profile of v0, /device:TPU:0, one launch (start us, length us, event | category | flops | bytes accessed | tf_op | source)
XLA Modules:
  0.0 1073.6 jit_solution(3452140487380955168)
XLA Ops:
  9.4 2.1 fusion.34
  18.1 3.2 constant_dynamic-update-slice_fusion.2
  23.4 18.8 %all-gather.11.cloned.1.call-done = bf16[256,2048]{1,0:T(8,128)(2,1)} async-done(((bf16[64,2048]{1,0:T(8,128)(2,1)}), bf16[256,2048]{1,0:T(8,128)(2,1)}) %all-gather.11.cloned.1.call-update) | async-done | bytes 1048592 | tf_op jit(solution)/shard_map/all_gather | solution.py:121
  42.3 3.8 fusion.110
  47.8 24.1 %all-gather.15.cloned.1.call-done = bf16[256,2048]{1,0:T(8,128)(2,1)} async-done(((bf16[64,2048]{1,0:T(8,128)(2,1)}), bf16[256,2048]{1,0:T(8,128)(2,1)}) %all-gather.15.cloned.1.call-update) | async-done | bytes 1048592 | tf_op jit(solution)/shard_map/all_gather | solution.py:121
  71.9 3.8 fusion.113
  82.0 2.2 multiply_multiply_fusion.1
  85.8 1.9 reshape.535
  87.7 2.0 multiply_reduce_fusion.15
  101.0 2.1 fusion.111
  112.0 2.1 fusion.114
  114.8 31.8 %reduce-scatter.13.cloned.1.call-done = f32[64,2048]{1,0:T(8,128)} async-done(((f32[256,2048]{1,0:T(8,128)}), f32[64,2048]{1,0:T(8,128)}) %reduce-scatter.13.cloned.1.call-update) | async-done | bytes 524304 | tf_op jit(solution)/shard_map/reduce_scatter | solution.py:149
  146.6 45.5 %reduce-scatter.17.cloned.1.call-done = f32[64,2048]{1,0:T(8,128)} async-done(((f32[256,2048]{1,0:T(8,128)}), f32[64,2048]{1,0:T(8,128)}) %reduce-scatter.17.cloned.1.call-update) | async-done | bytes 524304 | tf_op jit(solution)/shard_map/reduce_scatter | solution.py:149
  192.1 2.9 multiply_reduce_fusion.10
  196.7 1.9 fusion.107
  198.8 6.0 constant_dynamic-update-slice_fusion.4
  204.8 5.9 constant_dynamic-update-slice_fusion.3
  210.8 13.3 %all-gather.13.cloned.1.call-done = bf16[256,2048]{1,0:T(8,128)(2,1)} async-done(((bf16[64,2048]{1,0:T(8,128)(2,1)}), bf16[256,2048]{1,0:T(8,128)(2,1)}) %all-gather.13.cloned.1.call-update) | async-done | bytes 1048592 | tf_op jit(solution)/shard_map/all_gather | solution.py:156
  224.0 10.0 fusion.112
  234.0 19.5 %all-gather.23.cloned.1.call-done = bf16[1,1,256,2048]{3,2,1,0:T(8,128)(2,1)} async-done(((bf16[1,1,64,2048]{3,2,1,0:T(8,128)(2,1)}), bf16[1,1,256,2048]{3,2,1,0:T(8,128)(2,1)}) %all-gather.23.cloned.1.call-update) | async-done | bytes 1048592 | tf_op jit(solution)/shard_map/all_gather | solution.py:171
  253.5 7.2 multiply_convert_fusion.3
  261.9 9.4 fusion.21
  272.5 42.3 %reduce-scatter.21.cloned.1.call-done = f32[64,2048]{1,0:T(8,128)} async-done(((f32[256,2048]{1,0:T(8,128)}), f32[64,2048]{1,0:T(8,128)}) %reduce-scatter.21.cloned.1.call-update) | async-done | bytes 524304 | tf_op jit(solution)/shard_map/reduce_scatter | solution.py:178
  314.8 2.9 multiply_reduce_fusion.3
  318.9 26.2 %all-gather.17.cloned.1.call-done = bf16[256,2048]{1,0:T(8,128)(2,1)} async-done(((bf16[64,2048]{1,0:T(8,128)(2,1)}), bf16[256,2048]{1,0:T(8,128)(2,1)}) %all-gather.17.cloned.1.call-update) | async-done | bytes 1048592 | tf_op jit(solution)/shard_map/all_gather | solution.py:156
  345.1 10.0 fusion.115
  355.1 19.1 %all-gather.25.cloned.1.call-done = bf16[1,1,256,2048]{3,2,1,0:T(8,128)(2,1)} async-done(((bf16[1,1,64,2048]{3,2,1,0:T(8,128)(2,1)}), bf16[1,1,256,2048]{3,2,1,0:T(8,128)(2,1)}) %all-gather.25.cloned.1.call-update) | async-done | bytes 1048592 | tf_op jit(solution)/shard_map/all_gather | solution.py:171
  374.2 7.2 multiply_convert_fusion.1
  382.6 9.4 fusion.19
  392.1 5.8 convolution_convert_fusion
  399.1 36.4 %reduce-scatter.25.cloned.1.call-done = f32[64,2048]{1,0:T(8,128)} async-done(((f32[256,2048]{1,0:T(8,128)}), f32[64,2048]{1,0:T(8,128)}) %reduce-scatter.25.cloned.1.call-update) | async-done | bytes 524304 | tf_op jit(solution)/shard_map/reduce_scatter | solution.py:178
  435.5 2.0 multiply_reduce_fusion.2
  438.1 26.9 %reduce-scatter.19.cloned.1.call-done = bf16[64,2048]{1,0:T(8,128)(2,1)} async-done(((bf16[256,2048]{1,0:T(8,128)(2,1)}), bf16[64,2048]{1,0:T(8,128)(2,1)}) %reduce-scatter.19.cloned.1.call-update) | async-done | bytes 262160 | tf_op jit(solution)/shard_map/reduce_scatter | solution.py:163
  464.9 2.9 fusion.99
  473.6 21.0 %all-gather.19.cloned.1.call-done = bf16[256,2048]{1,0:T(8,128)(2,1)} async-done(((bf16[64,2048]{1,0:T(8,128)(2,1)}), bf16[256,2048]{1,0:T(8,128)(2,1)}) %all-gather.19.cloned.1.call-update) | async-done | bytes 1048592 | tf_op jit(solution)/shard_map/all_gather | solution.py:186
  494.6 2.7 convolution_convert_fusion.3
  497.3 1.8 copy.291
  499.1 2.3 fusion.10
  501.4 3.3 multiply_reduce_fusion.1
  504.7 19.0 %all-gather.21.cloned.1.call-done = bf16[256,2048]{1,0:T(8,128)(2,1)} async-done(((bf16[64,2048]{1,0:T(8,128)(2,1)}), bf16[256,2048]{1,0:T(8,128)(2,1)}) %all-gather.21.cloned.1.call-update) | async-done | bytes 1048592 | tf_op jit(solution)/shard_map/all_gather | solution.py:186
  523.7 2.7 convolution_convert_fusion.2
  537.8 2.4 multiply_reduce_fusion.13
  544.3 1.9 copy.285
  549.1 4.4 multiply_reduce_fusion.6
  556.5 4.8 fusion.76
  570.8 4.9 fusion.74
  575.8 5.7 convolution_convert_fusion.1
  581.6 2.3 fusion.75
  583.9 4.6 convolution_add_fusion.2
  589.7 11.6 %fusion.20 = f32[2048,3072]{1,0:T(8,128)} fusion(bf16[256,2048]{1,0:T(8,128)(2,1)S(1)} %copy-done.44, bf16[256,1536]{1,0:T(8,128)(2,1)} %copy-done.67, bf16[256,1536]{1,0:T(8,128)(2,1)} %copy-done.66), kind=kOutput, calls=%fused_computation.62 | convolution fusion | flops 3224371200 | bytes 27787264 | tf_op jit(solution)/shard_map/dot_general | solution.py:51
  601.3 16.9 %convolution_add_fusion = f32[2048,3072]{1,0:T(8,128)} fusion(f32[2048,3072]{1,0:T(8,128)} %fusion.20, bf16[256,2048]{1,0:T(8,128)(2,1)S(1)} %copy-done.40, bf16[256,1536]{1,0:T(8,128)(2,1)} %copy-done.64, bf16[256,1536]{1,0:T(8,128)(2,1)S(1)} %copy-done.63), kind=kOutput, calls=%fused_computation | convolution fusion | flops 3230662656 | bytes 52953088 | tf_op jit(solution)/shard_map/dot_general | solution.py:51
  620.3 2.8 convolution_add_fusion.3
  624.3 3.0 fusion.15
  627.3 6.5 convolution_add_fusion.1
  634.6 15.6 %reduce-scatter.27.cloned.1.call-done = f32[64,2048]{1,0:T(8,128)} async-done(((f32[256,2048]{1,0:T(8,128)}), f32[64,2048]{1,0:T(8,128)}) %reduce-scatter.27.cloned.1.call-update) | async-done | bytes 524304 | tf_op jit(solution)/shard_map/reduce_scatter | solution.py:220
  651.9 41.1 %all-reduce = (f32[2048]{0:T(1024)}, f32[128]{0:T(128)}, f32[128]{0:T(128)}, f32[2048]{0:T(1024)}) all-reduce(f32[2048]{0:T(1024)S(1)} %add.226, f32[128]{0:T(128)S(1)} %add.228, f32[128]{0:T(128)S(1)} %add.229, f32[2048]{0:T(1024)S(1)} %add.231), channel_id=1, replica_groups=mesh['wide'=8,'narrow'=4] {'wide','narrow'}, use_global_device_ids=true, to_apply=%region_38.39 | all-reduce | flops 4352 | bytes 34816 | tf_op jit(solution)/shard_map/psum | solution.py:241
  693.1 1.8 fusion.39
  697.4 56.1 %reduce-scatter.29.cloned.1.call-done = f32[256,1024]{1,0:T(8,128)} async-done(((f32[2048,1024]{1,0:T(8,128)}), f32[256,1024]{1,0:T(8,128)}) %reduce-scatter.29.cloned.1.call-update) | async-done | bytes 1048592 | tf_op jit(solution)/shard_map/reduce_scatter | solution.py:236
  753.5 1.9 slice.176
  755.4 2.0 fusion.102
  757.4 157.0 %reduce-scatter.33.cloned.1.call-done = f32[256,3072]{1,0:T(8,128)} async-done(((f32[2048,3072]{1,0:T(8,128)}), f32[256,3072]{1,0:T(8,128)}) %reduce-scatter.33.cloned.1.call-update) | async-done | bytes 3145744 | tf_op jit(solution)/shard_map/reduce_scatter | solution.py:237
  914.3 3.7 fusion.101
  918.1 51.9 %reduce-scatter.31.cloned.1.call-done = f32[512,256]{1,0:T(8,128)} async-done(((f32[512,2048]{1,0:T(8,128)}), f32[512,256]{1,0:T(8,128)}) %reduce-scatter.31.cloned.1.call-update) | async-done | bytes 524304 | tf_op jit(solution)/shard_map/reduce_scatter | solution.py:238
  970.0 96.3 %reduce-scatter.35.cloned.1.call-done = f32[1536,256]{1,0:T(8,128)} async-done(((f32[1536,2048]{1,0:T(8,128)}), f32[1536,256]{1,0:T(8,128)}) %reduce-scatter.35.cloned.1.call-update) | async-done | bytes 1572880 | tf_op jit(solution)/shard_map/reduce_scatter | solution.py:239
  (370 shorter events, 95.4 us)
Async XLA Ops:
  7.2 93.8 %copy-start = (bf16[512,2048]{1,0:T(8,128)(2,1)S(1)}, bf16[512,2048]{1,0:T(8,128)(2,1)}, u32[]{:S(2)}) copy-start(bf16[512,2048]{1,0:T(8,128)(2,1)} %param.22) | copy-start | bytes 6291460
  7.2 35.1 %all-gather.11.cloned.1.call-start = ((), (), s32[]{:S(2)}) async-start(), calls=%async_computation.12 | async-start | bytes 1310720 | tf_op jit(solution)/shard_map/all_gather | solution.py:121
  9.4 11.9 %copy-start.57 = (bf16[2048,256]{1,0:T(8,128)(2,1)S(1)}, bf16[2048,256]{1,0:T(8,128)(2,1)}, u32[]{:S(2)}) copy-start(bf16[2048,256]{1,0:T(8,128)(2,1)} %param.18) | copy-start | bytes 3145732
  11.5 60.4 %all-gather.15.cloned.1.call-start = ((), (), s32[]{:S(2)}) async-start(), calls=%async_computation.16 | async-start | bytes 1310720 | tf_op jit(solution)/shard_map/all_gather | solution.py:121
  12.2 134.4 %reduce-scatter.13.cloned.1.call-start = ((), (), s32[]{:S(2)}) async-start(), calls=%async_computation.13 | async-start | bytes 2621440 | tf_op jit(solution)/shard_map/reduce_scatter | solution.py:149
  13.0 69.0 %copy-start.98 = (f32[128]{0:T(128)}, f32[128]{0:T(128)S(1)}, u32[]{:S(2)}) copy-start(f32[128]{0:T(128)S(1)} %convert_element_type.147) | copy-start | bytes 1540
  15.6 76.6 %copy-start.102 = (f32[128]{0:T(128)}, f32[128]{0:T(128)S(1)}, u32[]{:S(2)}) copy-start(f32[128]{0:T(128)S(1)} %convert_element_type.145) | copy-start | bytes 1540
  46.0 31.4 %copy-start.20 = (f32[256,1024]{1,0:T(8,128)}, f32[256,1024]{1,0:T(8,128)S(1)}, u32[]{:S(2)}) copy-start(f32[256,1024]{1,0:T(8,128)S(1)} %fusion.110) | copy-start | bytes 3145732
  79.3 6.3 copy-start.8
  81.6 6.1 copy-start.10
  85.7 13.0 %copy-start.27 = (bf16[256,4,64]{2,0,1:T(8,128)(2,1)}, bf16[256,4,64]{2,0,1:T(8,128)(2,1)S(1)}, u32[]{:S(2)}) copy-start(bf16[256,4,64]{2,0,1:T(8,128)(2,1)S(1)} %copy.206) | copy-start | bytes 393220
  85.8 13.0 %copy-start.29 = (bf16[256,4,64]{2,0,1:T(8,128)(2,1)}, bf16[256,4,64]{2,0,1:T(8,128)(2,1)S(1)}, u32[]{:S(2)}) copy-start(bf16[256,4,64]{2,0,1:T(8,128)(2,1)S(1)} %copy.205) | copy-start | bytes 393220
  90.6 380.7 %copy-start.83 = (f32[256,2]{0,1:T(2,128)}, f32[256,2]{0,1:T(2,128)S(1)}, u32[]{:S(2)}) copy-start(f32[256,2]{0,1:T(2,128)S(1)} %add_rsqrt_fusion.3) | copy-start | bytes 6148
  103.1 89.0 %reduce-scatter.17.cloned.1.call-start = ((), (), s32[]{:S(2)}) async-start(), calls=%async_computation.17 | async-start | bytes 2621440 | tf_op jit(solution)/shard_map/reduce_scatter | solution.py:149
  103.2 5.3 copy-start.45
  114.1 110.0 %all-gather.13.cloned.1.call-start = ((), (), s32[]{:S(2)}) async-start(), calls=%async_computation.14 | async-start | bytes 1310720 | tf_op jit(solution)/shard_map/all_gather | solution.py:156
  196.6 56.9 %all-gather.23.cloned.1.call-start = ((), (), s32[]{:S(2)}) async-start(), calls=%async_computation.30 | async-start | bytes 1310720 | tf_op jit(solution)/shard_map/all_gather | solution.py:171
  198.6 116.2 %reduce-scatter.21.cloned.1.call-start = ((), (), s32[]{:S(2)}) async-start(), calls=%async_computation.20 | async-start | bytes 2621440 | tf_op jit(solution)/shard_map/reduce_scatter | solution.py:178
  271.2 73.9 %all-gather.17.cloned.1.call-start = ((), (), s32[]{:S(2)}) async-start(), calls=%async_computation.18 | async-start | bytes 1310720 | tf_op jit(solution)/shard_map/all_gather | solution.py:156
  317.7 56.5 %all-gather.25.cloned.1.call-start = ((), (), s32[]{:S(2)}) async-start(), calls=%async_computation.31 | async-start | bytes 1310720 | tf_op jit(solution)/shard_map/all_gather | solution.py:171
  318.4 117.1 %reduce-scatter.25.cloned.1.call-start = ((), (), s32[]{:S(2)}) async-start(), calls=%async_computation.23 | async-start | bytes 2621440 | tf_op jit(solution)/shard_map/reduce_scatter | solution.py:178
  392.0 72.9 %reduce-scatter.19.cloned.1.call-start = ((), (), s32[]{:S(2)}) async-start(), calls=%async_computation.19 | async-start | bytes 1310720 | tf_op jit(solution)/shard_map/reduce_scatter | solution.py:163
  397.9 96.7 %all-gather.19.cloned.1.call-start = ((), (), s32[]{:S(2)}) async-start(), calls=%async_computation.21 | async-start | bytes 1310720 | tf_op jit(solution)/shard_map/all_gather | solution.py:186
  467.9 55.8 %all-gather.21.cloned.1.call-start = ((), (), s32[]{:S(2)}) async-start(), calls=%async_computation.24 | async-start | bytes 1310720 | tf_op jit(solution)/shard_map/all_gather | solution.py:186
  468.6 166.0 %reduce-scatter.23.cloned.1.call-start = ((), (), s32[]{:S(2)}) async-start(), calls=%async_computation.22 | async-start | bytes 2621440 | tf_op jit(solution)/shard_map/reduce_scatter | solution.py:220
  532.3 5.4 copy-start.22
  532.3 5.4 copy-start.23
  532.4 5.4 copy-start.82
  532.8 8.2 copy-start.37
  536.6 5.6 copy-start.38
  543.1 6.0 copy-start.9
  543.1 6.0 copy-start.11
  547.6 5.9 copy-start.76
  549.0 5.2 copy-start.21
  549.1 5.8 copy-start.34
  549.1 6.5 copy-start.86
  556.5 5.9 copy-start.26
  561.3 7.1 copy-start.19
  561.3 7.1 copy-start.59
  561.3 8.6 copy-start.36
  561.3 88.9 %reduce-scatter.27.cloned.1.call-start = ((), (), s32[]{:S(2)}) async-start(), calls=%async_computation.25 | async-start | bytes 2621440 | tf_op jit(solution)/shard_map/reduce_scatter | solution.py:220
  575.7 117.3 %reduce-scatter.15.cloned.1.call-start = ((), (), s32[]{:S(2)}) async-start(), calls=%async_computation.15 | async-start | bytes 1310720 | tf_op jit(solution)/shard_map/reduce_scatter | solution.py:163
  575.8 5.8 copy-start.43
  575.8 5.8 copy-start.69
  581.5 172.0 %reduce-scatter.29.cloned.1.call-start = ((), (), s32[]{:S(2)}) async-start(), calls=%async_computation.26 | async-start | bytes 9437184 | tf_op jit(solution)/shard_map/reduce_scatter | solution.py:236
  588.5 12.8 %copy-start.40 = (bf16[256,2048]{1,0:T(8,128)(2,1)S(1)}, bf16[256,2048]{1,0:T(8,128)(2,1)}, u32[]{:S(2)}) copy-start(bf16[256,2048]{1,0:T(8,128)(2,1)} %all-gather.17.cloned.1.call-done) | copy-start | bytes 3145732
  588.5 12.8 %copy-start.63 = (bf16[256,1536]{1,0:T(8,128)(2,1)S(1)}, bf16[256,1536]{1,0:T(8,128)(2,1)}, u32[]{:S(2)}) copy-start(bf16[256,1536]{1,0:T(8,128)(2,1)} %copy-done.62) | copy-start | bytes 2359300
  588.5 325.8 %reduce-scatter.33.cloned.1.call-start = ((), (), s32[]{:S(2)}) async-start(), calls=%async_computation.28 | async-start | bytes 28311552 | tf_op jit(solution)/shard_map/reduce_scatter | solution.py:237
  618.3 351.7 %reduce-scatter.31.cloned.1.call-start = ((), (), s32[]{:S(2)}) async-start(), calls=%async_computation.27 | async-start | bytes 4718592 | tf_op jit(solution)/shard_map/reduce_scatter | solution.py:238
  623.1 443.2 %reduce-scatter.35.cloned.1.call-start = ((), (), s32[]{:S(2)}) async-start(), calls=%async_computation.29 | async-start | bytes 14155776 | tf_op jit(solution)/shard_map/reduce_scatter | solution.py:239
  633.8 16.4 %copy-start.4 = (bf16[2,1,64,2048]{3,2,1,0:T(8,128)(2,1)S(1)}, bf16[2,1,64,2048]{3,2,1,0:T(8,128)(2,1)}, u32[]{:S(2)}) copy-start(bf16[2,1,64,2048]{3,2,1,0:T(8,128)(2,1)} %param.14) | copy-start | bytes 1572868
  633.8 16.4 %copy-start.79 = (f32[2048]{0:T(1024)S(1)}, f32[2048]{0:T(1024)}, u32[]{:S(2)}) copy-start(f32[2048]{0:T(1024)} %copy-done.78) | copy-start | bytes 24580
  633.8 16.4 %copy-start.91 = (f32[64]{0:T(128)S(1)}, f32[64]{0:T(128)}, u32[]{:S(2)}) copy-start(f32[64]{0:T(128)} %copy-done.90) | copy-start | bytes 772
  633.8 16.4 %copy-start.93 = (f32[64]{0:T(128)S(1)}, f32[64]{0:T(128)}, u32[]{:S(2)}) copy-start(f32[64]{0:T(128)} %copy-done.92) | copy-start | bytes 772
  633.9 59.2 %copy-start.7 = (f32[64,2048]{1,0:T(8,128)S(1)}, f32[64,2048]{1,0:T(8,128)}, u32[]{:S(2)}) copy-start(f32[64,2048]{1,0:T(8,128)} %copy-done.6) | copy-start | bytes 1572868
  633.9 59.2 %copy-start.12 = (bf16[2,1,64,2048]{3,2,1,0:T(8,128)(2,1)S(1)}, bf16[2,1,64,2048]{3,2,1,0:T(8,128)(2,1)}, u32[]{:S(2)}) copy-start(bf16[2,1,64,2048]{3,2,1,0:T(8,128)(2,1)} %param.27) | copy-start | bytes 1572868
  633.9 59.2 %copy-start.15 = (f32[64,2048]{1,0:T(8,128)S(1)}, f32[64,2048]{1,0:T(8,128)}, u32[]{:S(2)}) copy-start(f32[64,2048]{1,0:T(8,128)} %reduce-scatter.21.cloned.1.call-done) | copy-start | bytes 1572868
  633.9 59.2 %copy-start.97 = (f32[64]{0:T(128)S(1)}, f32[64]{0:T(128)}, u32[]{:S(2)}) copy-start(f32[64]{0:T(128)} %copy-done.96) | copy-start | bytes 772
  633.9 59.2 %copy-start.101 = (f32[64]{0:T(128)S(1)}, f32[64]{0:T(128)}, u32[]{:S(2)}) copy-start(f32[64]{0:T(128)} %broadcast_multiply_fusion.7) | copy-start | bytes 772
  651.8 44.1 %copy-start.5 = (f32[64,2048]{1,0:T(8,128)S(1)}, f32[64,2048]{1,0:T(8,128)}, u32[]{:S(2)}) copy-start(f32[64,2048]{1,0:T(8,128)} %get-tuple-element.154) | copy-start | bytes 1572868
  651.9 44.1 %copy-start.14 = (f32[64,2048]{1,0:T(8,128)S(1)}, f32[64,2048]{1,0:T(8,128)}, u32[]{:S(2)}) copy-start(f32[64,2048]{1,0:T(8,128)} %reduce-scatter.25.cloned.1.call-done) | copy-start | bytes 1572868
  651.9 44.1 %copy-start.95 = (f32[64]{0:T(128)S(1)}, f32[64]{0:T(128)}, u32[]{:S(2)}) copy-start(f32[64]{0:T(128)} %add_rsqrt_fusion.4) | copy-start | bytes 772
  651.9 44.1 %copy-start.100 = (f32[64]{0:T(128)S(1)}, f32[64]{0:T(128)}, u32[]{:S(2)}) copy-start(f32[64]{0:T(128)} %broadcast_multiply_fusion.5) | copy-start | bytes 772
  755.4 311.0 %copy-start.1 = (bf16[512,2048]{1,0:T(8,128)(2,1)S(1)}, bf16[512,2048]{1,0:T(8,128)(2,1)}, u32[]{:S(2)}) copy-start(bf16[512,2048]{1,0:T(8,128)(2,1)} %param.22) | copy-start | bytes 6291460
  (60 other events, 140.3 us)
Sparse Core Ops, SparseCore 0:
  11.6 30.6 all-gather.10
  44.4 27.4 all-gather.14
  103.2 43.3 reduce-scatter.12
  148.8 43.1 reduce-scatter.16
  196.8 27.2 all-gather.12
  226.0 27.4 all-gather.22
  271.4 43.3 reduce-scatter.20
  317.8 27.2 all-gather.16
  346.8 27.4 all-gather.24
  392.1 43.3 reduce-scatter.24
  438.4 26.4 reduce-scatter.18
  468.0 26.5 all-gather.18
  496.3 27.4 all-gather.20
  561.4 43.3 reduce-scatter.22
  607.0 43.1 reduce-scatter.26
  653.0 27.1 reduce-scatter.14
  683.5 69.9 reduce-scatter.28
  757.4 156.8 reduce-scatter.32
  918.6 51.3 reduce-scatter.30
  973.9 92.3 reduce-scatter.34
where the time goes:
time: 1080 us; the launch traced here: 1070 us
  waiting for transfers between devices  723 us (67%)
  matrix products  156 us (14%)
  local copies, waits for them, and re-layouts  73.9 us (7%)
  other arithmetic  61.7 us (6%)
  blocking collectives  41.1 us (4%)
  between operations  16.1 us (1%)
    reduce_scatter x1, waiting for transfers between devices, local(): lax.psum_scatter(totals[1], 'wide', scatter_dimension=0, tiled=True)  157 us
    reduce_scatter x1, waiting for transfers between devices, local(): lax.psum_scatter(totals[3], 'wide', scatter_dimension=1, tiled=True)  96.3 us
    reduce_scatter x2, waiting for transfers between devices, local(): lax.psum_scatter(row_back_product(d_both, w_both), 'narrow', scatter_dime...  78.7 us
    reduce_scatter x2, waiting for transfers between devices, local(): lax.psum_scatter(row_product(attn_mix, w_out), 'narrow', scatter_dimensio...  77.3 us
    reduce_scatter x1, waiting for transfers between devices, local(): lax.psum_scatter(totals[0], 'wide', scatter_dimension=0, tiled=True)  56.1 us
    reduce_scatter x1, waiting for transfers between devices, local(): lax.psum_scatter(totals[2], 'wide', scatter_dimension=1, tiled=True)  51.9 us
    dot_general x8, matrix products, contract_rows(): lax.dot_general(left_side, right_side, (((0,), (0,)), ((), ())), preferre...  48.3 us
    dot_general x8, matrix products, contract_cols(): lax.dot_general(left_side, right_side, (((1,), (1,)), ((), ())), preferre...  48.1 us
  transfers between devices with their start and end apart: 20, of which 18 were waited for; matrix products, arithmetic and copies ran while one was open for 16% of the time, Pallas kernels for 0%

commit v1 on v0

--- a/solution.py
+++ b/solution.py
@@ -1,3 +1,4 @@
+import functools
 import jax
 import jax.numpy as jnp
 from jax import lax
@@ -5,6 +6,22 @@
 
 norm_eps = 1e-06
 masked_score = -1e30
+
+
+def _balance_levels_all(t0, named_axis):
+    width = lax.axis_size(named_axis)
+    line_up = [(rr, (rr + 1) % width) for rr in range(width)]
+    aux = [None] * width
+    aux[width - 1] = t0
+    for s in range(width - 2, -1, -1):
+        aux[s] = lax.ppermute(aux[s + 1], named_axis, line_up)
+    f_next = jnp.concatenate(aux, axis=0)
+    next_value = lax.axis_index(named_axis)
+    last = jnp.roll(f_next, (next_value + 1) * t0.shape[0], axis=0)
+    return last
+
+
+lanes_start = functools.partial(_balance_levels_all, named_axis="narrow")
 
 
 def rms_scale(values):
@@ -118,7 +135,7 @@
         scale_one = rms_scale(rows_in)
         hat_one = rows_in * scale_one
         normed = (hat_one * attn_gain_f).astype(jnp.bfloat16)
-        normed_full = lax.all_gather(normed, "narrow", axis=0, tiled=True)
+        normed_full = lanes_start(normed)
         projected = jnp.dot(normed_full, w_qkv, preferred_element_type=jnp.float32)
         query_raw = projected[:, :query_cols].reshape(seq_len, query_heads, head_dim)
         key_raw = projected[:, query_cols : query_cols + key_cols].reshape(

time: 1080 us -> 1050 us (0.972)
  waiting for transfers between devices: 723 us -> 705 us
    all_gather x2 -> x0, waiting for transfers between devices: 42.9 us -> none  [local(): normed_full = lax.all_gather(normed, 'narrow', axis=0, tiled=True)]
    ppermute x0 -> x6, waiting for transfers between devices: none -> 21.1 us  [_balance_levels_all(): aux[s] = lax.ppermute(aux[s + 1], named_axis, line_up)]
    unnamed x217 -> x263, local copies, waits for them, and re-layouts: 27.1 us -> 25.9 us
  transfers between devices with their start and end apart: 20 -> 24, of which waited for: 18 -> 21; matrix products, arithmetic and copies ran while one was open for 16% -> 15% of each run, Pallas kernels for 0% -> 0%
where the time goes in v1:
time: 1050 us; the launch traced here: 1040 us
  waiting for transfers between devices  705 us (67%)
  matrix products  147 us (14%)
  local copies, waits for them, and re-layouts  68.5 us (7%)
  other arithmetic  57 us (5%)
  blocking collectives  41.1 us (4%)
  between operations  16.1 us (2%)
    reduce_scatter x1, waiting for transfers between devices, local(): lax.psum_scatter(totals[1], 'wide', scatter_dimension=0, tiled=True)  157 us
    reduce_scatter x1, waiting for transfers between devices, local(): lax.psum_scatter(totals[3], 'wide', scatter_dimension=1, tiled=True)  96.4 us
    reduce_scatter x2, waiting for transfers between devices, local(): lax.psum_scatter(row_back_product(d_both, w_both), 'narrow', scatter_dime...  78.6 us
    reduce_scatter x2, waiting for transfers between devices, local(): lax.psum_scatter(row_product(attn_mix, w_out), 'narrow', scatter_dimensio...  78.1 us
    reduce_scatter x1, waiting for transfers between devices, local(): lax.psum_scatter(totals[0], 'wide', scatter_dimension=0, tiled=True)  56 us
    reduce_scatter x1, waiting for transfers between devices, local(): lax.psum_scatter(totals[2], 'wide', scatter_dimension=1, tiled=True)  51.7 us
    dot_general x8, matrix products, contract_rows(): lax.dot_general(left_side, right_side, (((0,), (0,)), ((), ())), preferre...  48.4 us
    dot_general x8, matrix products, contract_cols(): lax.dot_general(left_side, right_side, (((1,), (1,)), ((), ())), preferre...  43.7 us
  transfers between devices with their start and end apart: 24, of which 21 were waited for; matrix products, arithmetic and copies ran while one was open for 15% of the time, Pallas kernels for 0%

profile of v1, /device:TPU:0, one launch (start us, length us, event | category | flops | bytes accessed | tf_op | source)
XLA Modules:
  0.0 1042.0 jit_solution(16921173284426232183)
XLA Ops:
  10.6 3.1 collective-permute-start
  17.2 2.0 constant_dynamic-update-slice_fusion.2
  19.3 3.5 collective-permute-done
  24.8 3.7 collective-permute-done.3
  28.5 5.7 collective-permute-done.1
  34.9 2.3 constant_dynamic-update-slice_fusion
  37.3 2.5 collective-permute-done.4
  39.8 5.7 collective-permute-done.2
  45.5 3.7 fusion.22
  49.3 3.9 fusion.124
  54.2 3.7 fusion.15
  64.4 2.5 multiply_multiply_fusion.1
  77.2 2.1 fusion.125
  87.6 2.1 fusion.128
  90.4 32.5 %reduce-scatter.13.cloned.1.call-done = f32[64,2048]{1,0:T(8,128)} async-done(((f32[256,2048]{1,0:T(8,128)}), f32[64,2048]{1,0:T(8,128)}) %reduce-scatter.13.cloned.1.call-update) | async-done | bytes 524304 | tf_op jit(solution)/shard_map/reduce_scatter | solution.py:166
  122.9 45.6 %reduce-scatter.17.cloned.1.call-done = f32[64,2048]{1,0:T(8,128)} async-done(((f32[256,2048]{1,0:T(8,128)}), f32[64,2048]{1,0:T(8,128)}) %reduce-scatter.17.cloned.1.call-update) | async-done | bytes 524304 | tf_op jit(solution)/shard_map/reduce_scatter | solution.py:166
  168.5 2.9 multiply_reduce_fusion.10
  173.2 1.9 fusion.121
  175.6 6.0 constant_dynamic-update-slice_fusion.4
  181.6 6.0 constant_dynamic-update-slice_fusion.3
  187.6 13.0 %all-gather.9.cloned.1.call-done = bf16[256,2048]{1,0:T(8,128)(2,1)} async-done(((bf16[64,2048]{1,0:T(8,128)(2,1)}), bf16[256,2048]{1,0:T(8,128)(2,1)}) %all-gather.9.cloned.1.call-update) | async-done | bytes 1048592 | tf_op jit(solution)/shard_map/all_gather | solution.py:173
  200.5 9.9 fusion.126
  210.5 18.9 %all-gather.17.cloned.1.call-done = bf16[1,1,256,2048]{3,2,1,0:T(8,128)(2,1)} async-done(((bf16[1,1,64,2048]{3,2,1,0:T(8,128)(2,1)}), bf16[1,1,256,2048]{3,2,1,0:T(8,128)(2,1)}) %all-gather.17.cloned.1.call-update) | async-done | bytes 1048592 | tf_op jit(solution)/shard_map/all_gather | solution.py:188
  229.4 7.2 multiply_convert_fusion.3
  237.8 9.3 fusion.35
  248.3 42.3 %reduce-scatter.21.cloned.1.call-done = f32[64,2048]{1,0:T(8,128)} async-done(((f32[256,2048]{1,0:T(8,128)}), f32[64,2048]{1,0:T(8,128)}) %reduce-scatter.21.cloned.1.call-update) | async-done | bytes 524304 | tf_op jit(solution)/shard_map/reduce_scatter | solution.py:195
  290.6 2.9 multiply_reduce_fusion.3
  294.5 26.4 %all-gather.11.cloned.1.call-done = bf16[256,2048]{1,0:T(8,128)(2,1)} async-done(((bf16[64,2048]{1,0:T(8,128)(2,1)}), bf16[256,2048]{1,0:T(8,128)(2,1)}) %all-gather.11.cloned.1.call-update) | async-done | bytes 1048592 | tf_op jit(solution)/shard_map/all_gather | solution.py:173
  321.0 9.9 fusion.129
  330.9 19.2 %all-gather.19.cloned.1.call-done = bf16[1,1,256,2048]{3,2,1,0:T(8,128)(2,1)} async-done(((bf16[1,1,64,2048]{3,2,1,0:T(8,128)(2,1)}), bf16[1,1,256,2048]{3,2,1,0:T(8,128)(2,1)}) %all-gather.19.cloned.1.call-update) | async-done | bytes 1048592 | tf_op jit(solution)/shard_map/all_gather | solution.py:188
  350.1 7.3 multiply_convert_fusion.1
  358.5 9.4 fusion.33
  367.9 5.8 convolution_convert_fusion
  375.0 36.3 %reduce-scatter.25.cloned.1.call-done = f32[64,2048]{1,0:T(8,128)} async-done(((f32[256,2048]{1,0:T(8,128)}), f32[64,2048]{1,0:T(8,128)}) %reduce-scatter.25.cloned.1.call-update) | async-done | bytes 524304 | tf_op jit(solution)/shard_map/reduce_scatter | solution.py:195
  411.3 2.0 multiply_reduce_fusion.2
  413.8 26.9 %reduce-scatter.19.cloned.1.call-done = bf16[64,2048]{1,0:T(8,128)(2,1)} async-done(((bf16[256,2048]{1,0:T(8,128)(2,1)}), bf16[64,2048]{1,0:T(8,128)(2,1)}) %reduce-scatter.19.cloned.1.call-update) | async-done | bytes 262160 | tf_op jit(solution)/shard_map/reduce_scatter | solution.py:180
  440.7 2.9 fusion.113
  449.3 21.1 %all-gather.13.cloned.1.call-done = bf16[256,2048]{1,0:T(8,128)(2,1)} async-done(((bf16[64,2048]{1,0:T(8,128)(2,1)}), bf16[256,2048]{1,0:T(8,128)(2,1)}) %all-gather.13.cloned.1.call-update) | async-done | bytes 1048592 | tf_op jit(solution)/shard_map/all_gather | solution.py:203
  470.4 2.7 convolution_convert_fusion.3
  474.9 2.4 fusion.10
  477.3 2.9 multiply_reduce_fusion.1
  480.2 19.3 %all-gather.15.cloned.1.call-done = bf16[256,2048]{1,0:T(8,128)(2,1)} async-done(((bf16[64,2048]{1,0:T(8,128)(2,1)}), bf16[256,2048]{1,0:T(8,128)(2,1)}) %all-gather.15.cloned.1.call-update) | async-done | bytes 1048592 | tf_op jit(solution)/shard_map/all_gather | solution.py:203
  499.6 2.7 convolution_convert_fusion.2
  510.5 2.5 multiply_reduce_fusion.13
  520.8 3.4 multiply_reduce_fusion.6
  527.3 2.6 fusion.90
  536.7 2.6 fusion.88
  540.5 5.7 convolution_convert_fusion.1
  546.3 2.3 fusion.89
  548.6 4.6 convolution_add_fusion.2
  554.5 11.6 %fusion.34 = f32[2048,3072]{1,0:T(8,128)} fusion(bf16[256,2048]{1,0:T(8,128)(2,1)S(1)} %copy-done.49, bf16[256,1536]{1,0:T(8,128)(2,1)} %copy-done.82, bf16[256,1536]{1,0:T(8,128)(2,1)} %copy-done.81), kind=kOutput, calls=%fused_computation.92 | convolution fusion | flops 3224371200 | bytes 27787264 | tf_op jit(solution)/shard_map/dot_general | solution.py:68
  566.1 17.1 %convolution_add_fusion = f32[2048,3072]{1,0:T(8,128)} fusion(f32[2048,3072]{1,0:T(8,128)} %fusion.34, bf16[256,2048]{1,0:T(8,128)(2,1)S(1)} %copy-done.46, bf16[256,1536]{1,0:T(8,128)(2,1)} %copy-done.79, bf16[256,1536]{1,0:T(8,128)(2,1)S(1)} %copy-done.78), kind=kOutput, calls=%fused_computation | convolution fusion | flops 3230662656 | bytes 52953088 | tf_op jit(solution)/shard_map/dot_general | solution.py:68
  585.2 2.8 convolution_add_fusion.3
  589.2 3.0 fusion.29
  592.1 6.5 convolution_add_fusion.1
  599.4 19.5 %reduce-scatter.27.cloned.1.call-done = f32[64,2048]{1,0:T(8,128)} async-done(((f32[256,2048]{1,0:T(8,128)}), f32[64,2048]{1,0:T(8,128)}) %reduce-scatter.27.cloned.1.call-update) | async-done | bytes 524304 | tf_op jit(solution)/shard_map/reduce_scatter | solution.py:237
  620.6 41.1 %all-reduce = (f32[2048]{0:T(1024)}, f32[128]{0:T(128)}, f32[128]{0:T(128)}, f32[2048]{0:T(1024)}) all-reduce(f32[2048]{0:T(1024)S(1)} %add.239, f32[128]{0:T(128)S(1)} %add.241, f32[128]{0:T(128)S(1)} %add.242, f32[2048]{0:T(1024)S(1)} %add.244), channel_id=1, replica_groups=mesh['wide'=8,'narrow'=4] {'wide','narrow'}, use_global_device_ids=true, to_apply=%region_38.40 | all-reduce | flops 4352 | bytes 34816 | tf_op jit(solution)/shard_map/psum | solution.py:258
  666.2 56.0 %reduce-scatter.29.cloned.1.call-done = f32[256,1024]{1,0:T(8,128)} async-done(((f32[2048,1024]{1,0:T(8,128)}), f32[256,1024]{1,0:T(8,128)}) %reduce-scatter.29.cloned.1.call-update) | async-done | bytes 1048592 | tf_op jit(solution)/shard_map/reduce_scatter | solution.py:253
  722.3 1.9 slice.176
  724.1 2.0 fusion.116
  726.1 157.0 %reduce-scatter.33.cloned.1.call-done = f32[256,3072]{1,0:T(8,128)} async-done(((f32[2048,3072]{1,0:T(8,128)}), f32[256,3072]{1,0:T(8,128)}) %reduce-scatter.33.cloned.1.call-update) | async-done | bytes 3145744 | tf_op jit(solution)/shard_map/reduce_scatter | solution.py:254
  883.1 3.7 fusion.115
  886.8 51.7 %reduce-scatter.31.cloned.1.call-done = f32[512,256]{1,0:T(8,128)} async-done(((f32[512,2048]{1,0:T(8,128)}), f32[512,256]{1,0:T(8,128)}) %reduce-scatter.31.cloned.1.call-update) | async-done | bytes 524304 | tf_op jit(solution)/shard_map/reduce_scatter | solution.py:255
  938.6 96.4 %reduce-scatter.35.cloned.1.call-done = f32[1536,256]{1,0:T(8,128)} async-done(((f32[1536,2048]{1,0:T(8,128)}), f32[1536,256]{1,0:T(8,128)}) %reduce-scatter.35.cloned.1.call-update) | async-done | bytes 1572880 | tf_op jit(solution)/shard_map/reduce_scatter | solution.py:256
  (424 shorter events, 90.0 us)
Async XLA Ops:
  7.2 70.0 %copy-start = (bf16[512,2048]{1,0:T(8,128)(2,1)S(1)}, bf16[512,2048]{1,0:T(8,128)(2,1)}, u32[]{:S(2)}) copy-start(bf16[512,2048]{1,0:T(8,128)(2,1)} %param.24) | copy-start | bytes 6291460
  7.2 115.7 %reduce-scatter.13.cloned.1.call-start = ((), (), s32[]{:S(2)}) async-start(), calls=%async_computation.12 | async-start | bytes 2621440 | tf_op jit(solution)/shard_map/reduce_scatter | solution.py:166
  8.1 5.6 copy-start.97
  9.3 4.3 copy-start.110
  9.3 5.9 copy-start.112
  10.6 12.2 %collective-permute-start = (bf16[64,2048]{1,0:T(8,128)(2,1)S(1)}, bf16[64,2048]{1,0:T(8,128)(2,1)S(1)}, u32[]{:S(2)}, u32[]{:S(2)}) collective-permute-start(bf16[64,2048]{1,0:T(8,128)(2,1)S(1)} %get-tuple-element.137), channel_id=1, source_target_pairs={{0,1},{1,2},{2,3},{3,0},{4,5},{5,6},{6,7},{7,4},{8,9},{9,10},{10,1... | collective-permute-start | bytes 786440 | tf_op jit(solution)/shard_map/ppermute | solution.py:17
  13.7 14.8 %collective-permute-start.3 = (bf16[64,2048]{1,0:T(8,128)(2,1)S(1)}, bf16[64,2048]{1,0:T(8,128)(2,1)S(1)}, u32[]{:S(2)}, u32[]{:S(2)}) collective-permute-start(bf16[64,2048]{1,0:T(8,128)(2,1)S(1)} %get-tuple-element.138), channel_id=1, source_target_pairs={{0,1},{1,2},{2,3},{3,0},{4,5},{5,6},{6,7},{7,4},{8,9},{9,10},{10,1... | collective-permute-start | bytes 786440 | tf_op jit(solution)/shard_map/ppermute | solution.py:17
  17.2 7.4 copy-start.73
  19.2 15.7 %copy-start.125 = (bf16[128]{0:T(256)(128)(2,1)S(1)}, bf16[128]{0:T(256)(128)(2,1)}, u32[]{:S(2)}) copy-start(bf16[128]{0:T(256)(128)(2,1)} %param.22) | copy-start | bytes 772
  19.3 15.7 %copy-start.126 = (bf16[128]{0:T(256)(128)(2,1)S(1)}, bf16[128]{0:T(256)(128)(2,1)}, u32[]{:S(2)}) copy-start(bf16[128]{0:T(256)(128)(2,1)} %param.23) | copy-start | bytes 772
  22.8 11.3 %collective-permute-start.1 = (bf16[64,2048]{1,0:T(8,128)(2,1)S(1)}, bf16[64,2048]{1,0:T(8,128)(2,1)}, u32[]{:S(2)}, u32[]{:S(2)}) collective-permute-start(bf16[64,2048]{1,0:T(8,128)(2,1)S(1)} %collective-permute-done), channel_id=1, source_target_pairs={{0,1},{1,2},{2,3},{3,0},{4,5},{5,6},{6,7},{7,4},{8,9},{9,10},{10,1... | collective-permute-start | bytes 786440 | tf_op jit(solution)/shard_map/ppermute | solution.py:17
  28.4 20.8 %copy-start.96 = (bf16[64,2048]{1,0:T(8,128)(2,1)}, bf16[64,2048]{1,0:T(8,128)(2,1)S(1)}, u32[]{:S(2)}) copy-start(bf16[64,2048]{1,0:T(8,128)(2,1)S(1)} %collective-permute-done.3) | copy-start | bytes 786436
  28.4 11.3 %collective-permute-start.4 = (bf16[64,2048]{1,0:T(8,128)(2,1)S(1)}, bf16[64,2048]{1,0:T(8,128)(2,1)}, u32[]{:S(2)}, u32[]{:S(2)}) collective-permute-start(bf16[64,2048]{1,0:T(8,128)(2,1)S(1)} %collective-permute-done.3), channel_id=1, source_target_pairs={{0,1},{1,2},{2,3},{3,0},{4,5},{5,6},{6,7},{7,4},{8,9},{9,10},{10,1... | collective-permute-start | bytes 786440 | tf_op jit(solution)/shard_map/ppermute | solution.py:17
  34.1 11.4 %collective-permute-start.2 = (bf16[64,2048]{1,0:T(8,128)(2,1)}, bf16[64,2048]{1,0:T(8,128)(2,1)}, u32[]{:S(2)}, u32[]{:S(2)}) collective-permute-start(bf16[64,2048]{1,0:T(8,128)(2,1)} %collective-permute-done.1), channel_id=1, source_target_pairs={{0,1},{1,2},{2,3},{3,0},{4,5},{5,6},{6,7},{7,4},{8,9},{9,10},{10,1... | collective-permute-start | bytes 786440 | tf_op jit(solution)/shard_map/ppermute | solution.py:17
  34.9 29.5 %copy-start.118 = (f32[128]{0:T(128)}, f32[128]{0:T(128)S(1)}, u32[]{:S(2)}) copy-start(f32[128]{0:T(128)S(1)} %convert_element_type.147) | copy-start | bytes 1540
  34.9 37.1 %copy-start.122 = (f32[128]{0:T(128)}, f32[128]{0:T(128)S(1)}, u32[]{:S(2)}) copy-start(f32[128]{0:T(128)S(1)} %convert_element_type.145) | copy-start | bytes 1540
  39.8 14.4 %collective-permute-start.5 = (bf16[64,2048]{1,0:T(8,128)(2,1)}, bf16[64,2048]{1,0:T(8,128)(2,1)S(1)}, u32[]{:S(2)}, u32[]{:S(2)}) collective-permute-start(bf16[64,2048]{1,0:T(8,128)(2,1)} %collective-permute-done.4), channel_id=1, source_target_pairs={{0,1},{1,2},{2,3},{3,0},{4,5},{5,6},{6,7},{7,4},{8,9},{9,10},{10,1... | collective-permute-start | bytes 786440 | tf_op jit(solution)/shard_map/ppermute | solution.py:17
  49.2 8.6 copy-start.70
  53.2 7.8 copy-start.24
  61.8 5.2 copy-start.9
  66.9 5.1 copy-start.26
  66.9 5.1 copy-start.28
  70.5 376.6 %copy-start.102 = (f32[256,2]{0,1:T(2,128)}, f32[256,2]{0,1:T(2,128)S(1)}, u32[]{:S(2)}) copy-start(f32[256,2]{0,1:T(2,128)S(1)} %add_rsqrt_fusion.3) | copy-start | bytes 6148
  79.3 89.2 %reduce-scatter.17.cloned.1.call-start = ((), (), s32[]{:S(2)}) async-start(), calls=%async_computation.15 | async-start | bytes 2621440 | tf_op jit(solution)/shard_map/reduce_scatter | solution.py:166
  89.7 110.8 %all-gather.9.cloned.1.call-start = ((), (), s32[]{:S(2)}) async-start(), calls=%async_computation.13 | async-start | bytes 1310720 | tf_op jit(solution)/shard_map/all_gather | solution.py:173
  173.1 56.3 %all-gather.17.cloned.1.call-start = ((), (), s32[]{:S(2)}) async-start(), calls=%async_computation.28 | async-start | bytes 1310720 | tf_op jit(solution)/shard_map/all_gather | solution.py:188
  175.1 115.6 %reduce-scatter.21.cloned.1.call-start = ((), (), s32[]{:S(2)}) async-start(), calls=%async_computation.18 | async-start | bytes 2621440 | tf_op jit(solution)/shard_map/reduce_scatter | solution.py:195
  247.1 73.8 %all-gather.11.cloned.1.call-start = ((), (), s32[]{:S(2)}) async-start(), calls=%async_computation.16 | async-start | bytes 1310720 | tf_op jit(solution)/shard_map/all_gather | solution.py:173
  293.6 56.5 %all-gather.19.cloned.1.call-start = ((), (), s32[]{:S(2)}) async-start(), calls=%async_computation.29 | async-start | bytes 1310720 | tf_op jit(solution)/shard_map/all_gather | solution.py:188
  294.3 117.0 %reduce-scatter.25.cloned.1.call-start = ((), (), s32[]{:S(2)}) async-start(), calls=%async_computation.21 | async-start | bytes 2621440 | tf_op jit(solution)/shard_map/reduce_scatter | solution.py:195
  367.8 72.9 %reduce-scatter.19.cloned.1.call-start = ((), (), s32[]{:S(2)}) async-start(), calls=%async_computation.17 | async-start | bytes 1310720 | tf_op jit(solution)/shard_map/reduce_scatter | solution.py:180
  373.7 96.7 %all-gather.13.cloned.1.call-start = ((), (), s32[]{:S(2)}) async-start(), calls=%async_computation.19 | async-start | bytes 1310720 | tf_op jit(solution)/shard_map/all_gather | solution.py:203
  443.7 55.9 %all-gather.15.cloned.1.call-start = ((), (), s32[]{:S(2)}) async-start(), calls=%async_computation.22 | async-start | bytes 1310720 | tf_op jit(solution)/shard_map/all_gather | solution.py:203
  444.4 155.0 %reduce-scatter.23.cloned.1.call-start = ((), (), s32[]{:S(2)}) async-start(), calls=%async_computation.20 | async-start | bytes 2621440 | tf_op jit(solution)/shard_map/reduce_scatter | solution.py:237
  510.5 6.2 copy-start.42
  514.6 4.3 copy-start.53
  520.7 4.2 copy-start.25
  529.9 4.3 copy-start.23
  529.9 4.3 copy-start.74
  529.9 89.0 %reduce-scatter.27.cloned.1.call-start = ((), (), s32[]{:S(2)}) async-start(), calls=%async_computation.23 | async-start | bytes 2621440 | tf_op jit(solution)/shard_map/reduce_scatter | solution.py:237
  531.5 4.2 copy-start.40
  531.5 4.2 copy-start.106
  531.6 4.4 copy-start.88
  539.4 122.4 %reduce-scatter.15.cloned.1.call-start = ((), (), s32[]{:S(2)}) async-start(), calls=%async_computation.14 | async-start | bytes 1310720 | tf_op jit(solution)/shard_map/reduce_scatter | solution.py:180
  540.5 5.8 copy-start.16
  540.5 5.8 copy-start.84
  546.2 176.0 %reduce-scatter.29.cloned.1.call-start = ((), (), s32[]{:S(2)}) async-start(), calls=%async_computation.24 | async-start | bytes 9437184 | tf_op jit(solution)/shard_map/reduce_scatter | solution.py:253
  553.3 12.8 %copy-start.46 = (bf16[256,2048]{1,0:T(8,128)(2,1)S(1)}, bf16[256,2048]{1,0:T(8,128)(2,1)}, u32[]{:S(2)}) copy-start(bf16[256,2048]{1,0:T(8,128)(2,1)} %all-gather.11.cloned.1.call-done) | copy-start | bytes 3145732
  553.3 12.8 %copy-start.78 = (bf16[256,1536]{1,0:T(8,128)(2,1)S(1)}, bf16[256,1536]{1,0:T(8,128)(2,1)}, u32[]{:S(2)}) copy-start(bf16[256,1536]{1,0:T(8,128)(2,1)} %copy-done.77) | copy-start | bytes 2359300
  553.3 329.8 %reduce-scatter.33.cloned.1.call-start = ((), (), s32[]{:S(2)}) async-start(), calls=%async_computation.26 | async-start | bytes 28311552 | tf_op jit(solution)/shard_map/reduce_scatter | solution.py:254
  583.2 355.4 %reduce-scatter.31.cloned.1.call-start = ((), (), s32[]{:S(2)}) async-start(), calls=%async_computation.25 | async-start | bytes 4718592 | tf_op jit(solution)/shard_map/reduce_scatter | solution.py:255
  588.0 4.2 copy-start.37
  588.0 4.2 copy-start.65
  588.0 446.9 %reduce-scatter.35.cloned.1.call-start = ((), (), s32[]{:S(2)}) async-start(), calls=%async_computation.27 | async-start | bytes 14155776 | tf_op jit(solution)/shard_map/reduce_scatter | solution.py:256
  598.6 20.3 %copy-start.5 = (bf16[2,1,64,2048]{3,2,1,0:T(8,128)(2,1)S(1)}, bf16[2,1,64,2048]{3,2,1,0:T(8,128)(2,1)}, u32[]{:S(2)}) copy-start(bf16[2,1,64,2048]{3,2,1,0:T(8,128)(2,1)} %param.16) | copy-start | bytes 1572868
  598.6 20.3 %copy-start.98 = (f32[2048]{0:T(1024)S(1)}, f32[2048]{0:T(1024)}, u32[]{:S(2)}) copy-start(f32[2048]{0:T(1024)} %copy-done.97) | copy-start | bytes 24580
  598.6 20.3 %copy-start.111 = (f32[64]{0:T(128)S(1)}, f32[64]{0:T(128)}, u32[]{:S(2)}) copy-start(f32[64]{0:T(128)} %copy-done.110) | copy-start | bytes 772
  598.7 20.3 %copy-start.113 = (f32[64]{0:T(128)S(1)}, f32[64]{0:T(128)}, u32[]{:S(2)}) copy-start(f32[64]{0:T(128)} %copy-done.112) | copy-start | bytes 772
  598.7 63.1 %copy-start.8 = (f32[64,2048]{1,0:T(8,128)S(1)}, f32[64,2048]{1,0:T(8,128)}, u32[]{:S(2)}) copy-start(f32[64,2048]{1,0:T(8,128)} %copy-done.7) | copy-start | bytes 1572868
  598.7 63.1 %copy-start.17 = (bf16[2,1,64,2048]{3,2,1,0:T(8,128)(2,1)S(1)}, bf16[2,1,64,2048]{3,2,1,0:T(8,128)(2,1)}, u32[]{:S(2)}) copy-start(bf16[2,1,64,2048]{3,2,1,0:T(8,128)(2,1)} %param.29) | copy-start | bytes 1572868
  598.7 63.1 %copy-start.20 = (f32[64,2048]{1,0:T(8,128)S(1)}, f32[64,2048]{1,0:T(8,128)}, u32[]{:S(2)}) copy-start(f32[64,2048]{1,0:T(8,128)} %reduce-scatter.21.cloned.1.call-done) | copy-start | bytes 1572868
  598.7 63.1 %copy-start.117 = (f32[64]{0:T(128)S(1)}, f32[64]{0:T(128)}, u32[]{:S(2)}) copy-start(f32[64]{0:T(128)} %copy-done.116) | copy-start | bytes 772
  598.7 63.1 %copy-start.123 = (f32[64]{0:T(128)S(1)}, f32[64]{0:T(128)}, u32[]{:S(2)}) copy-start(f32[64]{0:T(128)} %broadcast_multiply_fusion.7) | copy-start | bytes 772
  724.1 310.8 %copy-start.1 = (bf16[512,2048]{1,0:T(8,128)(2,1)S(1)}, bf16[512,2048]{1,0:T(8,128)(2,1)}, u32[]{:S(2)}) copy-start(bf16[512,2048]{1,0:T(8,128)(2,1)} %param.24) | copy-start | bytes 6291460
  (87 other events, 170.3 us)
Sparse Core Ops, SparseCore 0:
  79.4 43.4 reduce-scatter.12
  125.3 43.1 reduce-scatter.16
  173.2 27.2 all-gather.8
  201.9 27.4 all-gather.16
  247.2 43.3 reduce-scatter.20
  293.7 27.2 all-gather.10
  322.6 27.4 all-gather.18
  368.0 43.3 reduce-scatter.24
  414.2 26.4 reduce-scatter.18
  443.8 26.5 all-gather.12
  472.1 27.4 all-gather.14
  530.0 43.3 reduce-scatter.22
  575.7 43.1 reduce-scatter.26
  621.7 27.1 reduce-scatter.14
  652.3 69.9 reduce-scatter.28
  726.2 156.8 reduce-scatter.32
  887.2 51.2 reduce-scatter.30
  942.5 92.3 reduce-scatter.34
